TPU v7x, 32 devices: a whole 2x2x4 slice. The times are simulated.
32 devices in a mesh: plane: 4 (over y, x), tile: 8 (over z, core).
Axes of the slice: x: 2, y: 2, z: 4, core: 2. Of those that a mesh axis runs over, the one named last changes fastest.
Arguments:
- recording: bfloat16 [4, 8, 3, 4, 256, 128], P('plane', 'tile'), may hold values from -8 to 8
- start_vectors: float32 [4, 16, 32, 128], P('plane', 'tile'), may hold values from -5 to 5
- footprints: bfloat16 [4, 1024, 256], P('plane', 'tile'), may hold values from 0.00019931793 to 0.029907227
- source_row: int32 [4, 1024, 1], P('plane', 'tile'), may hold values from 0 to 5; in each aligned block of 128 rows (0 to 127, 128 to 255, ..., all dimensions but the last counted through in order) at most 32 rows name the same one
- footprint_block: int32 [4, 1024], P('plane', 'tile'), may hold values from 0 to 3
Outputs:
- temporal_factors: float32 [4, 16, 32, 128], P('plane', 'tile')
- traces: float32 [4, 1024, 128], P('plane', 'tile')
Inputs may be any that keep to these rules, and one draw needn't show every extreme that they name: `source_row`: among the 128 sources of one device at most 32 share a value, and some value is shared by exactly 32 of them.
All inputs are finite; a program needn't handle non-finite values.
Results may differ from a plain program's by a relative error of at most 0.0069.
Values may be sent and summed in bfloat16 or wider, within the bound.
No kernel may reach another device: no remote copies, remote signals or barrier semaphores. Data moves between devices by JAX's collectives and lax.ppermute only.
A program may use at most 64 MiB of HBM per device.

v0:
```python
import jax
import jax.numpy as jnp
from jax import lax
from jax.sharding import PartitionSpec as P

ITERS = 3


def from_behind(block, axis, distance):
    devices = range(lax.axis_size(axis))
    route = [(i - distance, i) for i in devices if i - distance in devices]
    return lax.ppermute(block, axis, route)


def compress_patches(patches, start_block):
    temporal = start_block
    spatial = None
    for step_index in range(ITERS):
        projection = jnp.einsum(
            "prf,pkf->prk",
            temporal.astype(jnp.bfloat16),
            patches,
            preferred_element_type=jnp.float32,
        )
        gram_matrix = jnp.einsum(
            "prk,psk->prs", projection, projection, precision=lax.Precision.HIGHEST
        )
        cholesky_factor = jnp.linalg.cholesky(gram_matrix)
        spatial = jax.scipy.linalg.solve_triangular(cholesky_factor, projection, lower=True).astype(
            jnp.bfloat16
        )
        temporal = jnp.einsum("prk,pkf->prf", spatial, patches, preferred_element_type=jnp.float32)
    return (spatial, temporal)


def on_device(recording, start_vectors, footprints, source_row, footprint_block):
    tile_count = lax.axis_size("tile")
    own_strip = recording[0, 0]
    cell_count = own_strip.shape[0]
    patch_count = cell_count - 1
    block_pixels = own_strip.shape[2]
    frame_count = own_strip.shape[3]
    pixel_total = lax.axis_size("plane") * tile_count * cell_count * 4 * block_pixels
    frame_sum = jnp.sum(own_strip, axis=(0, 1, 2), dtype=jnp.float32)
    background = lax.psum(frame_sum, ("plane", "tile")) / pixel_total
    centered = (own_strip.astype(jnp.float32) - background).astype(jnp.bfloat16)
    lower_strip = from_behind(centered, "tile", -2)
    stacked = jnp.stack([centered, lower_strip])
    patches = jnp.stack(
        [
            stacked[:, column_index : column_index + 2].reshape(16 * block_pixels, frame_count)
            for column_index in range(patch_count)
        ]
    )
    spatial, temporal = compress_patches(patches, start_vectors[0])
    rank_width = spatial.shape[1]
    temporal_rounded = temporal.astype(jnp.bfloat16)
    source_rows = source_row[0, :, 0]
    block_value = footprint_block[0]
    footprint_rows = footprints[0]
    source_count = source_rows.shape[0]
    row_span = tile_count - 2
    capacity = max(2, (3 * source_count + 2 * row_span - 1) // (2 * row_span))
    row_match = (source_rows[:, None] == jnp.arange(tile_count)[None, :]).astype(jnp.int32)
    position = jnp.sum(jnp.cumsum(row_match, axis=0) * row_match, axis=1) - 1
    slot_upper = source_rows * capacity + position
    slot_lower = (source_rows + 2) * capacity + position
    footprint_send = jnp.zeros((tile_count * capacity, 2, block_pixels), jnp.bfloat16)
    footprint_send = (
        footprint_send.at[slot_upper, 0].set(footprint_rows).at[slot_lower, 1].set(footprint_rows)
    )
    block_send = jnp.full((tile_count * capacity, 2), -1, jnp.int32)
    block_send = block_send.at[slot_upper, 0].set(block_value).at[slot_lower, 1].set(block_value)
    footprint_send = footprint_send.reshape(tile_count, capacity, 2, block_pixels)
    block_send = block_send.reshape(tile_count, capacity, 2)
    spatial_blocks = spatial.reshape(patch_count, rank_width, 16, block_pixels)
    patch_axis = jnp.arange(patch_count)[None, None, :, None]
    block_axis = jnp.arange(8)[None, None, None, :]
    footprint_in = lax.all_to_all(footprint_send, "tile", split_axis=0, concat_axis=0, tiled=True)
    codes_in = lax.all_to_all(block_send, "tile", split_axis=0, concat_axis=0, tiled=True)
    role_terms = []
    for half_index in range(2):
        strip_offset = 1 - half_index
        block_range = spatial_blocks[:, :, strip_offset * 8 : strip_offset * 8 + 8]
        projected = jnp.einsum(
            "nkb,prgb->nkpgr",
            footprint_in[:, :, half_index],
            block_range,
            preferred_element_type=jnp.float32,
        )
        block_codes = codes_in[:, :, half_index]
        column_cell = (block_codes // 4 + 1)[:, :, None, None]
        quarter = (block_codes % 4)[:, :, None, None]
        filled = (block_codes >= 0)[:, :, None, None]
        from_left = (patch_axis == column_cell - 1) & (block_axis == quarter + 4)
        from_right = (patch_axis == column_cell) & (block_axis == quarter)
        selector = ((from_left | from_right) & filled).astype(jnp.float32)
        coefficient = jnp.sum(selector[..., None] * projected, axis=3)
        role_terms.append(
            coefficient.reshape(
                coefficient.shape[0], coefficient.shape[1], patch_count * rank_width
            )
        )
    coefficient = jnp.stack(role_terms, 2).astype(jnp.bfloat16)
    replies = lax.all_to_all(coefficient, "tile", split_axis=0, concat_axis=0, tiled=True)
    reply_rows = replies.reshape(tile_count * capacity, 2, patch_count * rank_width)
    upper_coefs = reply_rows[slot_upper, 0].reshape(source_count, patch_count, rank_width)
    lower_coefs = reply_rows[slot_lower, 1].reshape(source_count, patch_count, rank_width)
    coef_table = jnp.concatenate(
        [upper_coefs, lower_coefs, jnp.zeros((source_count, 1, rank_width), jnp.bfloat16)], 1
    )
    shard_rows = lax.all_gather(temporal_rounded, "tile", axis=0, tiled=True)
    patch_number = shard_rows.shape[0]
    patch_index = jnp.arange(patch_number)
    owner_row = patch_index // patch_count
    patch_column = patch_index % patch_count
    lookup = jnp.where(
        owner_row[None, :] == source_rows[:, None],
        patch_column[None, :],
        jnp.where(
            owner_row[None, :] == source_rows[:, None] + 2,
            patch_count + patch_column[None, :],
            2 * patch_count,
        ),
    )
    weights = jnp.take_along_axis(coef_table, lookup[:, :, None], axis=1)
    weights = weights.reshape(source_count, patch_number * rank_width)
    summed = jnp.dot(
        weights,
        shard_rows.reshape(patch_number * rank_width, frame_count),
        preferred_element_type=jnp.float32,
    )
    traces = 0.25 * summed
    return (temporal[None], traces[None])


def solution(mesh):
    placed = (
        P("plane", "tile", None, None, None, None),
        P("plane", "tile", None, None),
        P("plane", "tile", None),
        P("plane", "tile", None),
        P("plane", "tile"),
    )
    return jax.shard_map(
        on_device,
        mesh=mesh,
        in_specs=placed,
        out_specs=(P("plane", "tile", None, None), P("plane", "tile", None)),
        check_vma=False,
    )
```

profile of v0, /device:TPU:0, one launch (start us, length us, event | category | flops | bytes accessed | tf_op | source)
XLA Modules:
  0.0 174.9 jit_solution(6968167123436777132)
XLA Ops:
  0.6 1.6 convert_reduce_fusion
  2.3 42.0 %psum.7 = f32[128]{0:T(128)S(1)} all-reduce(f32[128]{0:T(128)S(1)} %convert_reduce_fusion), channel_id=1, replica_groups=mesh['plane'=4,'tile'=8] {'plane','tile'}, use_global_device_ids=true, to_apply=%region_1.0 | all-reduce | flops 128 | bytes 1024 | tf_op jit(solution)/shard_map/psum | solution.py:45
  44.3 0.2 fusion.5
  44.5 1.3 collective-permute-start
  45.9 0.2 reduce_window_sum.11
  46.1 0.2 select_reduce_fusion
  46.3 6.8 %scatter_fusion = s32[256,2]{0,1:T(2,128)S(1)} fusion(s32[256,2]{0,1:T(2,128)S(1)} %broadcast_in_dim.81, s32[128]{0:T(128)S(1)} %get-tuple-element.28, s32[128]{0:T(128)S(1)} %bitcast.186), kind=kCustom, calls=%fused_computation.3 | custom fusion | bytes 2560 | tf_op jit(solution)/shard_map/scatter | solution.py:73
  53.2 6.8 %scatter_fusion.1 = s32[256,2]{0,1:T(2,128)S(1)} fusion(s32[256,2]{0,1:T(2,128)S(1)} %scatter_fusion, s32[128]{0:T(128)S(1)} %get-tuple-element.29, s32[128]{0:T(128)S(1)} %bitcast.187), kind=kCustom, calls=%fused_computation.4 | custom fusion | bytes 2560 | tf_op jit(solution)/shard_map/scatter | solution.py:73
  60.1 0.6 copy.50
  60.7 5.7 %all-to-all-start = ((s32[8,32,2]{1,2,0:T(2,128)}), s32[8,32,2]{1,2,0:T(2,128)S(1)}, u32[]{:S(2)}, u32[]{:S(2)}) async-start(s32[8,32,2]{1,2,0:T(2,128)} %copy.50), calls=%async_computation | async-start | bytes 16384 | tf_op jit(solution)/shard_map/all_to_all | solution.py:80
  66.5 0.2 fusion.3
  66.9 0.1 broadcast_in_dim.82
  67.1 6.8 %scatter_fusion.2 = bf16[256,2,256]{2,1,0:T(2,128)(2,1)S(1)} fusion(bf16[256,2,256]{2,1,0:T(2,128)(2,1)S(1)} %broadcast_in_dim.82, s32[128]{0:T(128)S(1)} %get-tuple-element.28, bf16[128,256]{1,0:T(8,128)(2,1)S(1)} %bitcast.172), kind=kCustom, calls=%fused_computation.5 | custom fusion | bytes 197632 | tf_op jit(solution)/shard_map/scatter | solution.py:70
  73.9 6.8 %scatter_fusion.3 = bf16[256,2,256]{2,1,0:T(2,128)(2,1)S(1)} fusion(bf16[256,2,256]{2,1,0:T(2,128)(2,1)S(1)} %scatter_fusion.2, s32[128]{0:T(128)S(1)} %get-tuple-element.29, bf16[128,256]{1,0:T(8,128)(2,1)S(1)} %bitcast.173), kind=kCustom, calls=%fused_computation.6 | custom fusion | bytes 197632 | tf_op jit(solution)/shard_map/scatter | solution.py:70
  80.7 0.8 copy.52
  81.6 5.1 %all-to-all-start.1 = ((bf16[8,32,2,256]{3,1,2,0:T(8,128)(2,1)}), bf16[8,32,2,256]{3,1,2,0:T(8,128)(2,1)}, u32[]{:S(2)}, u32[]{:S(2)}) async-start(bf16[8,32,2,256]{3,1,2,0:T(8,128)(2,1)} %copy.52), calls=%async_computation.1 | async-start | bytes 524288 | tf_op jit(solution)/shard_map/all_to_all | solution.py:79
  87.0 0.7 and_convert_fusion.1
  87.6 0.2 fusion.10
  87.8 0.6 copy-done.7
  88.4 0.8 fusion.25
  89.2 1.1 fusion.41
  90.4 5.9 %custom-call.24 = f32[2,32,32]{2,1,0:T(8,128)S(1)} custom-call(f32[2,32,32]{2,1,0:T(8,128)S(1)} %fusion.24), custom_call_target="Cholesky" | custom-call | tf_op jit(solution)/shard_map/jit(cholesky)/cholesky | solution.py:28
  96.5 4.9 %custom-call.25 = f32[2,1,32,32]{2,3,1,0:T(8,128)S(1)} custom-call(f32[2,1,32,32]{3,2,1,0:T(8,128)S(1)} %select_bitcast_fusion.2), custom_call_target="InvertDiagBlocksLowerTriangular" | custom-call | tf_op jit(solution)/shard_map/jit(_solve_triangular)/vmap()/triangular_solve | solution.py:29
  101.4 1.1 convolution_convert_fusion.2
  102.5 2.7 %fusion.8 = f32[2,32,4096]{2,1,0:T(8,128)S(1)} fusion(bf16[2,32,4096]{2,1,0:T(8,128)(2,1)S(1)} %convolution_convert_fusion.2, bf16[1,4096,128]{2,1,0:T(8,128)(2,1)} %bitcast.165, bf16[1,4096,128]{2,1,0:T(8,128)(2,1)S(1)} %bitcast.161), kind=kOutput, calls=%fused_computation.29 | convolution fusion | flops 136323072 | bytes 3670016 | tf_op jit(solution)/shard_map/prf,pkf->prk/dot_general | solution.py:19
  105.2 1.1 fusion.42
  106.4 5.9 %custom-call.26 = f32[2,32,32]{2,1,0:T(8,128)S(1)} custom-call(f32[2,32,32]{2,1,0:T(8,128)S(1)} %fusion.22), custom_call_target="Cholesky" | custom-call | tf_op jit(solution)/shard_map/jit(cholesky)/cholesky | solution.py:28
  112.5 4.9 %custom-call.27 = f32[2,1,32,32]{2,3,1,0:T(8,128)S(1)} custom-call(f32[2,1,32,32]{3,2,1,0:T(8,128)S(1)} %select_bitcast_fusion.1), custom_call_target="InvertDiagBlocksLowerTriangular" | custom-call | tf_op jit(solution)/shard_map/jit(_solve_triangular)/vmap()/triangular_solve | solution.py:29
  117.4 1.1 convolution_convert_fusion.1
  118.5 2.7 %fusion.9 = f32[2,32,4096]{2,1,0:T(8,128)S(1)} fusion(bf16[2,32,4096]{2,1,0:T(8,128)(2,1)S(1)} %convolution_convert_fusion.1, bf16[1,4096,128]{2,1,0:T(8,128)(2,1)} %bitcast.166, bf16[1,4096,128]{2,1,0:T(8,128)(2,1)S(1)} %bitcast.162), kind=kOutput, calls=%fused_computation.30 | convolution fusion | flops 136323072 | bytes 3670016 | tf_op jit(solution)/shard_map/prf,pkf->prk/dot_general | solution.py:19
  121.2 1.1 fusion.43
  122.4 5.9 %custom-call.28 = f32[2,32,32]{2,1,0:T(8,128)S(1)} custom-call(f32[2,32,32]{2,1,0:T(8,128)S(1)} %fusion.20), custom_call_target="Cholesky" | custom-call | tf_op jit(solution)/shard_map/jit(cholesky)/cholesky | solution.py:28
  128.5 5.1 %custom-call.29 = f32[2,1,32,32]{2,3,1,0:T(8,128)S(1)} custom-call(f32[2,1,32,32]{3,2,1,0:T(8,128)S(1)} %select_bitcast_fusion), custom_call_target="InvertDiagBlocksLowerTriangular" | custom-call | tf_op jit(solution)/shard_map/jit(_solve_triangular)/vmap()/triangular_solve | solution.py:29
  133.6 1.0 convolution_convert_fusion
  134.8 1.7 fusion
  136.7 1.8 %fusion.1 = bf16[8,32,2,32]{1,0,3,2:T(8,128)(2,1)S(1)} fusion(f32[8,32,2,8]{1,3,0,2:T(8,128)S(1)} %copy-done.4, bf16[2,32,16,256]{3,2,1,0:T(8,128)(2,1)S(1)} %bitcast.170, bf16[8,32,2,256]{3,1,2,0:T(8,128)(2,1)} %all-to-all-done.1), kind=kOutput, calls=%fused_computation.17 | convolution fusion | flops 67354624 | bytes 491520 | tf_op jit(solution)/shard_map/nkb,prgb->nkpgr/dot_general | solution.py:85
  138.5 0.1 copy.70
  138.7 0.8 reshape.613
  139.5 5.1 %all-to-all-start.2 = ((bf16[8,2,2048]{2,1,0:T(2,128)(2,1)}), bf16[8,2,2048]{2,1,0:T(2,128)(2,1)S(1)}, u32[]{:S(2)}, u32[]{:S(2)}) async-start(bf16[8,2,2048]{2,1,0:T(2,128)(2,1)} %reshape.613), calls=%async_computation.2 | async-start | bytes 131072 | tf_op jit(solution)/shard_map/all_to_all | solution.py:105
  144.6 1.1 fusion.40
  145.7 14.5 %all_gather.3 = bf16[16,32,128]{2,1,0:T(8,128)(2,1)S(1)} all-gather(bf16[2,32,128]{2,1,0:T(8,128)(2,1)S(1)} %get-tuple-element.26), channel_id=1, replica_groups=mesh['plane'=4,'tile'=8] {'tile'}, dimensions={0}, use_global_device_ids=true | all-gather | bytes 147456 | tf_op jit(solution)/shard_map/all_gather | solution.py:112
  160.2 0.1 reshape.614
  160.4 1.0 gather_fusion.1
  161.6 1.0 gather_fusion
  162.8 0.2 copy.61
  163.0 10.6 %gather_fusion.2 = bf16[2048,32]{1,0:T(8,128)(2,1)S(1)} fusion(bf16[128,5,32]{2,0,1:T(8,128)(2,1)S(1)} %copy.61, s32[2048]{0:T(1024)S(1)} %reshape.577), kind=kCustom, calls=%fused_computation.2 | custom fusion | bytes 278528 | tf_op jit(solution)/shard_map/jit(take_along_axis)/gather | solution.py:126
  173.5 0.4 copy.62
  174.0 0.9 fusion.7
  (70 shorter events, 2.3 us)
Async XLA Ops:
  0.6 43.7 %copy-start = (bf16[1,1,3,4,256,128]{5,4,3,2,1,0:T(8,128)(2,1)S(1)}, bf16[1,1,3,4,256,128]{5,4,3,2,1,0:T(8,128)(2,1)}, u32[]{:S(2)}) copy-start(bf16[1,1,3,4,256,128]{5,4,3,2,1,0:T(8,128)(2,1)} %param.8) | copy-start | bytes 2359300
  0.6 45.2 %copy-start.5 = (s32[1,128,1]{1,2,0:T(1,128)S(1)}, s32[1,128,1]{1,2,0:T(1,128)}, u32[]{:S(2)}) copy-start(s32[1,128,1]{1,2,0:T(1,128)} %param.11) | copy-start | bytes 1540
  2.3 44.0 %copy-start.6 = (s32[1,128]{1,0:T(1,128)S(1)}, s32[1,128]{1,0:T(1,128)}, u32[]{:S(2)}) copy-start(s32[1,128]{1,0:T(1,128)} %param.12) | copy-start | bytes 1540
  44.5 43.1 %collective-permute-start = (bf16[3,4,256,128]{3,2,1,0:T(8,128)(2,1)S(1)}, bf16[3,4,256,128]{3,2,1,0:T(8,128)(2,1)S(1)}, u32[]{:S(2)}, u32[]{:S(2)}) collective-permute-start(bf16[3,4,256,128]{3,2,1,0:T(8,128)(2,1)S(1)} %fusion.5), channel_id=1, source_target_pairs={{2,0},{3,1},{4,2},{5,3},{6,4},{7,5},{10,8},{11,9},{12,10},{13,11},... | collective-permute-start | bytes 2359304 | tf_op jit(solution)/shard_map/ppermute | solution.py:12
  60.0 7.0 %copy-start.3 = (bf16[1,128,256]{2,1,0:T(8,128)(2,1)S(1)}, bf16[1,128,256]{2,1,0:T(8,128)(2,1)}, u32[]{:S(2)}) copy-start(bf16[1,128,256]{2,1,0:T(8,128)(2,1)} %param.10) | copy-start | bytes 196612
  60.7 20.9 %all-to-all-start = ((s32[8,32,2]{1,2,0:T(2,128)}), s32[8,32,2]{1,2,0:T(2,128)S(1)}, u32[]{:S(2)}, u32[]{:S(2)}) async-start(s32[8,32,2]{1,2,0:T(2,128)} %copy.50), calls=%async_computation | async-start | bytes 16384 | tf_op jit(solution)/shard_map/all_to_all | solution.py:80
  81.6 53.1 %all-to-all-start.1 = ((bf16[8,32,2,256]{3,1,2,0:T(8,128)(2,1)}), bf16[8,32,2,256]{3,1,2,0:T(8,128)(2,1)}, u32[]{:S(2)}, u32[]{:S(2)}) async-start(bf16[8,32,2,256]{3,1,2,0:T(8,128)(2,1)} %copy.52), calls=%async_computation.1 | async-start | bytes 524288 | tf_op jit(solution)/shard_map/all_to_all | solution.py:79
  87.6 0.8 copy-start.7
  87.8 1.4 copy-start.1
  134.8 1.9 %copy-start.4 = (f32[8,32,2,8]{1,3,0,2:T(8,128)S(1)}, f32[8,32,2,8]{1,3,0,2:T(8,128)}, u32[]{:S(2)}) copy-start(f32[8,32,2,8]{1,3,0,2:T(8,128)} %and_convert_fusion.1) | copy-start | bytes 49156
  136.7 7.9 %copy-start.2 = (bf16[2,2,4,256,128]{4,3,2,1,0:T(8,128)(2,1)S(1)}, bf16[2,2,4,256,128]{4,3,2,1,0:T(8,128)(2,1)}, u32[]{:S(2)}) copy-start(bf16[2,2,4,256,128]{4,3,2,1,0:T(8,128)(2,1)} %copy-done.1) | copy-start | bytes 3145732
  139.5 20.7 %all-to-all-start.2 = ((bf16[8,2,2048]{2,1,0:T(2,128)(2,1)}), bf16[8,2,2048]{2,1,0:T(2,128)(2,1)S(1)}, u32[]{:S(2)}, u32[]{:S(2)}) async-start(bf16[8,2,2048]{2,1,0:T(2,128)(2,1)} %reshape.613), calls=%async_computation.2 | async-start | bytes 131072 | tf_op jit(solution)/shard_map/all_to_all | solution.py:105
where the time goes:
time: 175 us
  blocking collectives  56.5 us (32%)
  local copies, waits for them, and re-layouts  44.8 us (26%)
  other arithmetic  37 us (21%)
  matrix products  18.2 us (10%)
  starting transfers between devices  17.2 us (10%)
    psum x1, blocking collectives, on_device(): background = lax.psum(frame_sum, ('plane', 'tile')) / pixel_total  42 us
    another operation x10, other arithmetic, compress_patches(): cholesky_factor = jnp.linalg.cholesky(gram_matrix)  18.1 us
    another operation x7, other arithmetic, compress_patches(): jax.scipy.linalg.solve_triangular(cholesky_factor, projection, lower=True)  15.2 us
    all_gather x1, blocking collectives, on_device(): shard_rows = lax.all_gather(temporal_rounded, 'tile', axis=0, tiled=True)  14.5 us
    scatter x2, local copies, waits for them, and re-layouts, on_device(): block_send.at[slot_upper, 0].set(block_value).at[slot_lower, 1]  13.7 us
    scatter x2, local copies, waits for them, and re-layouts, on_device(): footprint_send.at[slot_upper, 0].set(footprint_rows).at[slot_lower, 1]  13.6 us
    gather x3, local copies, waits for them, and re-layouts, on_device(): weights = jnp.take_along_axis(coef_table, lookup[:, :, None], axis=1)  11.1 us
    dot_general x3, matrix products, compress_patches(): jnp.einsum('prf,pkf->prk', temporal.astype(jnp.bfloat16), patches, prefer...  6.26 us
  transfers between devices with their start and end apart: 4, of which 0 were waited for; matrix products, arithmetic and copies ran while one was open for 45% of the time, Pallas kernels for 0%

commit v1 on v0

--- a/solution.py
+++ b/solution.py
@@ -102,7 +102,19 @@
             )
         )
     coefficient = jnp.stack(role_terms, 2).astype(jnp.bfloat16)
-    replies = lax.all_to_all(coefficient, "tile", split_axis=0, concat_axis=0, tiled=True)
+    ways, here = (lax.axis_size("tile"), lax.axis_index("tile"))
+    width = coefficient.shape[0] // ways
+    shape = list(coefficient.shape)
+    shape[0] = width
+    height = shape[0]
+    shape[0] = height * ways
+    full = jnp.zeros(shape, coefficient.dtype)
+    for mask in range(ways):
+        part = lax.dynamic_slice_in_dim(coefficient, (here ^ mask) * width, width, axis=0)
+        if mask:
+            part = lax.ppermute(part, "tile", [(d, d ^ mask) for d in range(ways)])
+        full = lax.dynamic_update_slice_in_dim(full, part, (here ^ mask) * height, axis=0)
+    replies = full
     reply_rows = replies.reshape(tile_count * capacity, 2, patch_count * rank_width)
     upper_coefs = reply_rows[slot_upper, 0].reshape(source_count, patch_count, rank_width)
     lower_coefs = reply_rows[slot_lower, 1].reshape(source_count, patch_count, rank_width)

time: 175 us -> 183 us (1.046)
  waiting for transfers between devices: 0.01 us -> 4.88 us
  starting transfers between devices: 17.2 us -> 20.4 us
    ppermute x0 -> x7, starting transfers between devices: none -> 8.31 us  [on_device(): part = lax.ppermute(part, 'tile', [(d, d ^ mask) for d in range(ways)])]
    all_to_all x1 -> x0, starting transfers between devices: 5.1 us -> none  [on_device(): lax.all_to_all(coefficient, 'tile', split_axis=0, concat_axis=0, tiled=True)]
    ppermute x0 -> x7, waiting for transfers between devices: none -> 4.87 us  [on_device(): part = lax.ppermute(part, 'tile', [(d, d ^ mask) for d in range(ways)])]
  transfers between devices with their start and end apart: 4 -> 10, of which waited for: 0 -> 2; matrix products, arithmetic and copies ran while one was open for 45% -> 43% of each run, Pallas kernels for 0% -> 0%
where the time goes in v1:
time: 183 us; the launch traced here: 182 us
  blocking collectives  56.8 us (31%)
  local copies, waits for them, and re-layouts  44 us (24%)
  other arithmetic  36.8 us (20%)
  starting transfers between devices  20.4 us (11%)
  matrix products  18.2 us (10%)
  waiting for transfers between devices  4.88 us (3%)
    psum x1, blocking collectives, on_device(): background = lax.psum(frame_sum, ('plane', 'tile')) / pixel_total  42 us
    another operation x10, other arithmetic, compress_patches(): cholesky_factor = jnp.linalg.cholesky(gram_matrix)  18.1 us
    another operation x7, other arithmetic, compress_patches(): jax.scipy.linalg.solve_triangular(cholesky_factor, projection, lower=True)  15 us
    all_gather x1, blocking collectives, on_device(): shard_rows = lax.all_gather(temporal_rounded, 'tile', axis=0, tiled=True)  14.7 us
    scatter x2, local copies, waits for them, and re-layouts, on_device(): block_send.at[slot_upper, 0].set(block_value).at[slot_lower, 1]  13.7 us
    scatter x2, local copies, waits for them, and re-layouts, on_device(): footprint_send.at[slot_upper, 0].set(footprint_rows).at[slot_lower, 1]  13.6 us
    gather x3, local copies, waits for them, and re-layouts, on_device(): weights = jnp.take_along_axis(coef_table, lookup[:, :, None], axis=1)  11.1 us
    ppermute x7, starting transfers between devices, on_device(): part = lax.ppermute(part, 'tile', [(d, d ^ mask) for d in range(ways)])  8.31 us
  transfers between devices with their start and end apart: 10, of which 2 were waited for; matrix products, arithmetic and copies ran while one was open for 43% of the time, Pallas kernels for 0%

profile of v1, /device:TPU:0, one launch (start us, length us, event | category | flops | bytes accessed | tf_op | source)
XLA Modules:
  0.0 182.3 jit_solution(1928909996321195826)
XLA Ops:
  0.6 1.6 convert_reduce_fusion
  2.3 42.0 %psum.7 = f32[128]{0:T(128)S(1)} all-reduce(f32[128]{0:T(128)S(1)} %convert_reduce_fusion), channel_id=1, replica_groups=mesh['plane'=4,'tile'=8] {'plane','tile'}, use_global_device_ids=true, to_apply=%region_1.0 | all-reduce | flops 128 | bytes 1024 | tf_op jit(solution)/shard_map/psum | solution.py:45
  44.3 0.2 fusion.5
  44.5 1.3 collective-permute-start
  46.3 6.8 %scatter_fusion = s32[256,2]{0,1:T(2,128)S(1)} fusion(s32[256,2]{0,1:T(2,128)S(1)} %broadcast_in_dim.85, s32[128]{0:T(128)S(1)} %fusion.41, s32[128]{0:T(128)S(1)} %bitcast.182), kind=kCustom, calls=%fused_computation.3 | custom fusion | bytes 2560 | tf_op jit(solution)/shard_map/scatter | solution.py:73
  53.2 6.8 %scatter_fusion.1 = s32[256,2]{0,1:T(2,128)S(1)} fusion(s32[256,2]{0,1:T(2,128)S(1)} %scatter_fusion, s32[128]{0:T(128)S(1)} %fusion.42, s32[128]{0:T(128)S(1)} %bitcast.183), kind=kCustom, calls=%fused_computation.4 | custom fusion | bytes 2560 | tf_op jit(solution)/shard_map/scatter | solution.py:73
  60.1 0.6 copy.63
  60.8 5.7 %all-to-all-start = ((s32[8,32,2]{1,2,0:T(2,128)}), s32[8,32,2]{1,2,0:T(2,128)S(1)}, u32[]{:S(2)}, u32[]{:S(2)}) async-start(s32[8,32,2]{1,2,0:T(2,128)} %copy.63), calls=%async_computation | async-start | bytes 16384 | tf_op jit(solution)/shard_map/all_to_all | solution.py:80
  66.5 0.2 fusion.3
  67.1 6.8 %scatter_fusion.2 = bf16[256,2,256]{2,1,0:T(2,128)(2,1)S(1)} fusion(bf16[256,2,256]{2,1,0:T(2,128)(2,1)S(1)} %broadcast_in_dim.86, s32[128]{0:T(128)S(1)} %fusion.41, bf16[128,256]{1,0:T(8,128)(2,1)S(1)} %bitcast.168), kind=kCustom, calls=%fused_computation.5 | custom fusion | bytes 197632 | tf_op jit(solution)/shard_map/scatter | solution.py:70
  74.0 6.8 %scatter_fusion.3 = bf16[256,2,256]{2,1,0:T(2,128)(2,1)S(1)} fusion(bf16[256,2,256]{2,1,0:T(2,128)(2,1)S(1)} %scatter_fusion.2, s32[128]{0:T(128)S(1)} %fusion.42, bf16[128,256]{1,0:T(8,128)(2,1)S(1)} %bitcast.169), kind=kCustom, calls=%fused_computation.6 | custom fusion | bytes 197632 | tf_op jit(solution)/shard_map/scatter | solution.py:70
  80.8 0.8 copy.65
  81.7 5.1 %all-to-all-start.1 = ((bf16[8,32,2,256]{3,1,2,0:T(8,128)(2,1)}), bf16[8,32,2,256]{3,1,2,0:T(8,128)(2,1)}, u32[]{:S(2)}, u32[]{:S(2)}) async-start(bf16[8,32,2,256]{3,1,2,0:T(8,128)(2,1)} %copy.65), calls=%async_computation.1 | async-start | bytes 524288 | tf_op jit(solution)/shard_map/all_to_all | solution.py:79
  87.0 0.7 and_convert_fusion
  87.7 0.2 fusion.10
  87.9 0.6 copy-done.7
  88.4 0.8 fusion.33
  89.2 1.1 fusion.49
  90.4 5.9 %custom-call.24 = f32[2,32,32]{2,1,0:T(8,128)S(1)} custom-call(f32[2,32,32]{2,1,0:T(8,128)S(1)} %fusion.24), custom_call_target="Cholesky" | custom-call | tf_op jit(solution)/shard_map/jit(cholesky)/cholesky | solution.py:28
  96.5 4.9 %custom-call.25 = f32[2,1,32,32]{2,3,1,0:T(8,128)S(1)} custom-call(f32[2,1,32,32]{3,2,1,0:T(8,128)S(1)} %select_bitcast_fusion.2), custom_call_target="InvertDiagBlocksLowerTriangular" | custom-call | tf_op jit(solution)/shard_map/jit(_solve_triangular)/vmap()/triangular_solve | solution.py:29
  101.4 1.1 convolution_convert_fusion.2
  102.5 2.7 %fusion.8 = f32[2,32,4096]{2,1,0:T(8,128)S(1)} fusion(bf16[2,32,4096]{2,1,0:T(8,128)(2,1)S(1)} %convolution_convert_fusion.2, bf16[1,4096,128]{2,1,0:T(8,128)(2,1)} %bitcast.162, bf16[1,4096,128]{2,1,0:T(8,128)(2,1)S(1)} %bitcast.158), kind=kOutput, calls=%fused_computation.29 | convolution fusion | flops 136323072 | bytes 3670016 | tf_op jit(solution)/shard_map/prf,pkf->prk/dot_general | solution.py:19
  105.2 1.1 fusion.50
  106.4 5.9 %custom-call.26 = f32[2,32,32]{2,1,0:T(8,128)S(1)} custom-call(f32[2,32,32]{2,1,0:T(8,128)S(1)} %fusion.22), custom_call_target="Cholesky" | custom-call | tf_op jit(solution)/shard_map/jit(cholesky)/cholesky | solution.py:28
  112.5 4.9 %custom-call.27 = f32[2,1,32,32]{2,3,1,0:T(8,128)S(1)} custom-call(f32[2,1,32,32]{3,2,1,0:T(8,128)S(1)} %select_bitcast_fusion.1), custom_call_target="InvertDiagBlocksLowerTriangular" | custom-call | tf_op jit(solution)/shard_map/jit(_solve_triangular)/vmap()/triangular_solve | solution.py:29
  117.4 1.1 convolution_convert_fusion.1
  118.5 2.7 %fusion.9 = f32[2,32,4096]{2,1,0:T(8,128)S(1)} fusion(bf16[2,32,4096]{2,1,0:T(8,128)(2,1)S(1)} %convolution_convert_fusion.1, bf16[1,4096,128]{2,1,0:T(8,128)(2,1)} %bitcast.163, bf16[1,4096,128]{2,1,0:T(8,128)(2,1)S(1)} %bitcast.159), kind=kOutput, calls=%fused_computation.30 | convolution fusion | flops 136323072 | bytes 3670016 | tf_op jit(solution)/shard_map/prf,pkf->prk/dot_general | solution.py:19
  121.2 1.1 fusion.51
  122.4 5.9 %custom-call.28 = f32[2,32,32]{2,1,0:T(8,128)S(1)} custom-call(f32[2,32,32]{2,1,0:T(8,128)S(1)} %fusion.20), custom_call_target="Cholesky" | custom-call | tf_op jit(solution)/shard_map/jit(cholesky)/cholesky | solution.py:28
  128.5 4.9 %custom-call.29 = f32[2,1,32,32]{2,3,1,0:T(8,128)S(1)} custom-call(f32[2,1,32,32]{3,2,1,0:T(8,128)S(1)} %select_bitcast_fusion), custom_call_target="InvertDiagBlocksLowerTriangular" | custom-call | tf_op jit(solution)/shard_map/jit(_solve_triangular)/vmap()/triangular_solve | solution.py:29
  133.4 1.1 convolution_convert_fusion
  134.7 1.1 fusion.48
  135.8 14.7 %all_gather.3 = bf16[16,32,128]{2,1,0:T(8,128)(2,1)S(1)} all-gather(bf16[2,32,128]{2,1,0:T(8,128)(2,1)S(1)} %get-tuple-element.34), channel_id=1, replica_groups=mesh['plane'=4,'tile'=8] {'tile'}, dimensions={0}, use_global_device_ids=true | all-gather | bytes 147456 | tf_op jit(solution)/shard_map/all_gather | solution.py:124
  150.5 1.8 fusion.1
  152.4 1.7 fusion
  154.3 0.4 collective-permute-start.1
  154.7 1.5 collective-permute-start.2
  156.3 2.3 %collective-permute-start.4 = (bf16[1,32,2,64]{3,1,0,2:T(8,128)(2,1)S(1)}, bf16[1,32,2,64]{3,1,0,2:T(8,128)(2,1)S(1)}, u32[]{:S(2)}, u32[]{:S(2)}) collective-permute-start(bf16[1,32,2,64]{3,1,0,2:T(8,128)(2,1)S(1)} %get-tuple-element.19), channel_id=1, source_target_pairs={{0,4},{1,5},{2,6},{3,7},{4,0},{5,1},{6,2},{7,3},{8,12},{9,13},{10,... | collective-permute-start | bytes 24584 | tf_op jit(solution)/shard_map/ppermute | solution.py:115
  158.6 0.6 collective-permute-start.5
  159.3 3.3 %collective-permute-start.6 = (bf16[1,32,2,64]{3,1,0,2:T(8,128)(2,1)S(1)}, bf16[1,32,2,64]{3,1,0,2:T(8,128)(2,1)S(1)}, u32[]{:S(2)}, u32[]{:S(2)}) collective-permute-start(bf16[1,32,2,64]{3,1,0,2:T(8,128)(2,1)S(1)} %get-tuple-element.20), channel_id=1, source_target_pairs={{0,6},{1,7},{2,4},{3,5},{4,2},{5,3},{6,0},{7,1},{8,14},{9,15},{10,... | collective-permute-start | bytes 24584 | tf_op jit(solution)/shard_map/ppermute | solution.py:115
  163.0 2.0 %collective-permute-done.6 = bf16[1,32,2,64]{3,1,0,2:T(8,128)(2,1)S(1)} collective-permute-done((bf16[1,32,2,64]{3,1,0,2:T(8,128)(2,1)S(1)}, bf16[1,32,2,64]{3,1,0,2:T(8,128)(2,1)S(1)}, u32[]{:S(2)}, u32[]{:S(2)}) %collective-permute-start.6) | collective-permute-done | bytes 8224 | tf_op jit(solution)/shard_map/ppermute | solution.py:115
  165.0 2.9 %collective-permute-done.7 = bf16[1,32,2,64]{3,1,0,2:T(8,128)(2,1)S(1)} collective-permute-done((bf16[1,32,2,64]{3,1,0,2:T(8,128)(2,1)S(1)}, bf16[1,32,2,64]{3,1,0,2:T(8,128)(2,1)S(1)}, u32[]{:S(2)}, u32[]{:S(2)}) %collective-permute-start.7) | collective-permute-done | bytes 8224 | tf_op jit(solution)/shard_map/ppermute | solution.py:115
  167.9 1.0 gather_fusion.1
  169.0 1.0 gather_fusion
  170.2 0.2 copy.80
  170.4 10.6 %gather_fusion.2 = bf16[2048,32]{1,0:T(8,128)(2,1)S(1)} fusion(bf16[128,5,32]{2,0,1:T(8,128)(2,1)S(1)} %copy.80, s32[2048]{0:T(1024)S(1)} %reshape.577), kind=kCustom, calls=%fused_computation.2 | custom fusion | bytes 278528 | tf_op jit(solution)/shard_map/jit(take_along_axis)/gather | solution.py:138
  181.0 0.4 copy.81
  181.4 0.9 fusion.7
  (88 shorter events, 3.3 us)
Async XLA Ops:
  0.6 43.7 %copy-start = (bf16[1,1,3,4,256,128]{5,4,3,2,1,0:T(8,128)(2,1)S(1)}, bf16[1,1,3,4,256,128]{5,4,3,2,1,0:T(8,128)(2,1)}, u32[]{:S(2)}) copy-start(bf16[1,1,3,4,256,128]{5,4,3,2,1,0:T(8,128)(2,1)} %param.8) | copy-start | bytes 2359300
  0.6 45.2 %copy-start.5 = (s32[1,128,1]{1,2,0:T(1,128)S(1)}, s32[1,128,1]{1,2,0:T(1,128)}, u32[]{:S(2)}) copy-start(s32[1,128,1]{1,2,0:T(1,128)} %param.11) | copy-start | bytes 1540
  2.3 44.1 %copy-start.6 = (s32[1,128]{1,0:T(1,128)S(1)}, s32[1,128]{1,0:T(1,128)}, u32[]{:S(2)}) copy-start(s32[1,128]{1,0:T(1,128)} %param.12) | copy-start | bytes 1540
  44.5 43.1 %collective-permute-start = (bf16[3,4,256,128]{3,2,1,0:T(8,128)(2,1)S(1)}, bf16[3,4,256,128]{3,2,1,0:T(8,128)(2,1)S(1)}, u32[]{:S(2)}, u32[]{:S(2)}) collective-permute-start(bf16[3,4,256,128]{3,2,1,0:T(8,128)(2,1)S(1)} %fusion.5), channel_id=1, source_target_pairs={{2,0},{3,1},{4,2},{5,3},{6,4},{7,5},{10,8},{11,9},{12,10},{13,11},... | collective-permute-start | bytes 2359304 | tf_op jit(solution)/shard_map/ppermute | solution.py:12
  60.1 7.1 %copy-start.3 = (bf16[1,128,256]{2,1,0:T(8,128)(2,1)S(1)}, bf16[1,128,256]{2,1,0:T(8,128)(2,1)}, u32[]{:S(2)}) copy-start(bf16[1,128,256]{2,1,0:T(8,128)(2,1)} %param.10) | copy-start | bytes 196612
  60.8 20.9 %all-to-all-start = ((s32[8,32,2]{1,2,0:T(2,128)}), s32[8,32,2]{1,2,0:T(2,128)S(1)}, u32[]{:S(2)}, u32[]{:S(2)}) async-start(s32[8,32,2]{1,2,0:T(2,128)} %copy.63), calls=%async_computation | async-start | bytes 16384 | tf_op jit(solution)/shard_map/all_to_all | solution.py:80
  81.7 68.8 %all-to-all-start.1 = ((bf16[8,32,2,256]{3,1,2,0:T(8,128)(2,1)}), bf16[8,32,2,256]{3,1,2,0:T(8,128)(2,1)}, u32[]{:S(2)}, u32[]{:S(2)}) async-start(bf16[8,32,2,256]{3,1,2,0:T(8,128)(2,1)} %copy.65), calls=%async_computation.1 | async-start | bytes 524288 | tf_op jit(solution)/shard_map/all_to_all | solution.py:79
  87.7 0.8 copy-start.7
  87.8 1.4 copy-start.1
  133.4 1.3 copy-start.2
  150.5 1.9 %copy-start.4 = (f32[8,32,2,8]{1,3,0,2:T(8,128)S(1)}, f32[8,32,2,8]{1,3,0,2:T(8,128)}, u32[]{:S(2)}) copy-start(f32[8,32,2,8]{1,3,0,2:T(8,128)} %and_convert_fusion) | copy-start | bytes 49156
  154.3 5.0 %collective-permute-start.1 = (bf16[1,32,2,64]{3,1,0,2:T(8,128)(2,1)S(1)}, bf16[1,32,2,64]{3,1,0,2:T(8,128)(2,1)S(1)}, u32[]{:S(2)}, u32[]{:S(2)}) collective-permute-start(bf16[1,32,2,64]{3,1,0,2:T(8,128)(2,1)S(1)} %get-tuple-element.16), channel_id=1, source_target_pairs={{0,1},{1,0},{2,3},{3,2},{4,5},{5,4},{6,7},{7,6},{8,9},{9,8},{10,11... | collective-permute-start | bytes 24584 | tf_op jit(solution)/shard_map/ppermute | solution.py:115
  154.7 8.0 %collective-permute-start.2 = (bf16[1,32,2,64]{3,1,0,2:T(8,128)(2,1)S(1)}, bf16[1,32,2,64]{3,1,0,2:T(8,128)(2,1)S(1)}, u32[]{:S(2)}, u32[]{:S(2)}) collective-permute-start(bf16[1,32,2,64]{3,1,0,2:T(8,128)(2,1)S(1)} %get-tuple-element.17), channel_id=1, source_target_pairs={{0,2},{1,3},{2,0},{3,1},{4,6},{5,7},{6,4},{7,5},{8,10},{9,11},{10,... | collective-permute-start | bytes 24584 | tf_op jit(solution)/shard_map/ppermute | solution.py:115
  156.2 6.6 %collective-permute-start.3 = (bf16[1,32,2,64]{3,1,0,2:T(8,128)(2,1)S(1)}, bf16[1,32,2,64]{3,1,0,2:T(8,128)(2,1)S(1)}, u32[]{:S(2)}, u32[]{:S(2)}) collective-permute-start(bf16[1,32,2,64]{3,1,0,2:T(8,128)(2,1)S(1)} %get-tuple-element.18), channel_id=1, source_target_pairs={{0,3},{1,2},{2,1},{3,0},{4,7},{5,6},{6,5},{7,4},{8,11},{9,10},{10,... | collective-permute-start | bytes 24584 | tf_op jit(solution)/shard_map/ppermute | solution.py:115
  156.3 6.6 %collective-permute-start.4 = (bf16[1,32,2,64]{3,1,0,2:T(8,128)(2,1)S(1)}, bf16[1,32,2,64]{3,1,0,2:T(8,128)(2,1)S(1)}, u32[]{:S(2)}, u32[]{:S(2)}) collective-permute-start(bf16[1,32,2,64]{3,1,0,2:T(8,128)(2,1)S(1)} %get-tuple-element.19), channel_id=1, source_target_pairs={{0,4},{1,5},{2,6},{3,7},{4,0},{5,1},{6,2},{7,3},{8,12},{9,13},{10,... | collective-permute-start | bytes 24584 | tf_op jit(solution)/shard_map/ppermute | solution.py:115
  158.6 4.3 %collective-permute-start.5 = (bf16[1,32,2,64]{3,1,0,2:T(8,128)(2,1)S(1)}, bf16[1,32,2,64]{3,1,0,2:T(8,128)(2,1)S(1)}, u32[]{:S(2)}, u32[]{:S(2)}) collective-permute-start(bf16[1,32,2,64]{3,1,0,2:T(8,128)(2,1)S(1)} %get-tuple-element.21), channel_id=1, source_target_pairs={{0,5},{1,4},{2,7},{3,6},{4,1},{5,0},{6,3},{7,2},{8,13},{9,12},{10,... | collective-permute-start | bytes 24584 | tf_op jit(solution)/shard_map/ppermute | solution.py:115
  159.3 5.6 %collective-permute-start.6 = (bf16[1,32,2,64]{3,1,0,2:T(8,128)(2,1)S(1)}, bf16[1,32,2,64]{3,1,0,2:T(8,128)(2,1)S(1)}, u32[]{:S(2)}, u32[]{:S(2)}) collective-permute-start(bf16[1,32,2,64]{3,1,0,2:T(8,128)(2,1)S(1)} %get-tuple-element.20), channel_id=1, source_target_pairs={{0,6},{1,7},{2,4},{3,5},{4,2},{5,3},{6,0},{7,1},{8,14},{9,15},{10,... | collective-permute-start | bytes 24584 | tf_op jit(solution)/shard_map/ppermute | solution.py:115
  162.7 5.1 %collective-permute-start.7 = (bf16[1,32,2,64]{3,1,0,2:T(8,128)(2,1)S(1)}, bf16[1,32,2,64]{3,1,0,2:T(8,128)(2,1)S(1)}, u32[]{:S(2)}, u32[]{:S(2)}) collective-permute-start(bf16[1,32,2,64]{3,1,0,2:T(8,128)(2,1)S(1)} %get-tuple-element.14), channel_id=1, source_target_pairs={{0,7},{1,6},{2,5},{3,4},{4,3},{5,2},{6,1},{7,0},{8,15},{9,14},{10,... | collective-permute-start | bytes 24584 | tf_op jit(solution)/shard_map/ppermute | solution.py:115
